TPU v7x, 512 devices: a whole 4x4x16 slice. The times are simulated.
512 devices in a mesh: dp: 8 (over x, core), expert: 64 (over z, y).
Axes of the slice: x: 4, y: 4, z: 16, core: 2. Of those that a mesh axis runs over, the one named last changes fastest.
Arguments:
- cells: bfloat16 [131072, 1024], P(('dp', 'expert')), may hold values from -6 to 6
- cell_bins: int32 [131072], P(('dp', 'expert')), may hold values from 0 to 127
- tile_counts: int32 [512, 8], P(('dp', 'expert')), may hold values from 1 to 96, 256 in all within a row
- bin_base: bfloat16 [65536, 1024], P(('dp', 'expert')), may hold values from -6 to 6
- norm_gain: float32 [1024], replicated, may hold values from 0.1 to 1.9
- expert_ids: int32 [65536, 1], P(('dp', 'expert')), may hold values from 0 to 63; in each aligned block of 128 rows (0 to 127, 128 to 255, ...) at most 3 rows name the same one
- gate_q: bfloat16 [64, 4096, 1024], P('expert', 'dp'), may hold values from -0.1875 to 0.1875
- up_q: bfloat16 [64, 4096, 1024], P('expert', 'dp'), may hold values from -0.1875 to 0.1875
- down_q: bfloat16 [64, 4096, 1024], P('expert', 'dp'), may hold values from -0.09375 to 0.09375
- gate_scales: int32 [64, 32, 8], P('expert', 'dp'), may hold values from -1 to 1
- up_scales: int32 [64, 32, 8], P('expert', 'dp'), may hold values from -1 to 1
- down_scales: int32 [64, 32, 8], P('expert', 'dp'), may hold values from -1 to 1
Outputs:
- encoded: bfloat16 [65536, 1024], P(('dp', 'expert'))
Inputs may be any that keep to these rules, and one draw needn't show every extreme that they name: Each device's cells are stored grouped by tile in order of t; row s of tile_counts gives the lengths of these groups, sums to 256, and its largest entry is 96. `expert_ids`: among the 128 bins of one tile no expert is named more than 3 times, a bound that some block reaches.
All inputs are finite; a program needn't handle non-finite values.
Results may differ from a plain program's by a relative error of at most 0.014.
Values may be sent and summed in bfloat16 or wider, within the bound.
No kernel may reach another device: no remote copies, remote signals or barrier semaphores. Data moves between devices by JAX's collectives and lax.ppermute only.
A program may use at most 64 MiB of HBM per device.

v0:
```python
import jax
import jax.numpy as jnp
from jax import lax
from jax.sharding import PartitionSpec as P

QB = 128


def dequantize(quant, scale):
    factor = jnp.exp2(scale.astype(jnp.float32))
    factor = jnp.repeat(jnp.repeat(factor, QB, axis=0), QB, axis=1).astype(jnp.bfloat16)
    return quant * factor


def on_device(
    cells,
    cell_bins,
    tile_counts,
    bin_base,
    norm_gain,
    expert_ids,
    gate_q,
    up_q,
    down_q,
    gate_scales,
    up_scales,
    down_scales,
):
    dp_size = lax.axis_size("dp")
    expert_count = lax.axis_size("expert") * gate_q.shape[0]
    cell_total = cells.shape[0]
    tile_bins = bin_base.shape[0]
    counts = tile_counts[0]
    run_ends = jnp.cumsum(counts)
    run_starts = run_ends - counts
    bin_iota = jnp.arange(tile_bins, dtype=jnp.int32)
    cell_cap = min(3 * cell_total // dp_size, cell_total - dp_size + 1)
    slot_iota = jnp.arange(cell_cap, dtype=jnp.int32)
    take_rows = jnp.clip(run_starts[:, None] + slot_iota[None, :], 0, cell_total - 1).reshape(-1)
    valid = (slot_iota[None, :] < counts[:, None]).reshape(-1)
    slot_rows = jnp.where(
        valid[:, None], jnp.take(cells, take_rows, axis=0), jnp.zeros((), jnp.bfloat16)
    )
    slot_bins = jnp.where(valid, jnp.take(cell_bins, take_rows), -1)
    got_rows, got_bins = (
        lax.all_to_all(slot_rows, "dp", split_axis=0, concat_axis=0, tiled=True),
        lax.all_to_all(slot_bins, "dp", split_axis=0, concat_axis=0, tiled=True),
    )
    matcher = (bin_iota[:, None] == got_bins[None, :]).astype(jnp.bfloat16)
    splat_sum = jnp.dot(matcher, got_rows, preferred_element_type=jnp.float32)
    residual_in = bin_base.astype(jnp.float32) + splat_sum
    mean_sq = jnp.mean(residual_in * residual_in, axis=1, keepdims=True)
    normed = (residual_in * lax.rsqrt(mean_sq + 1e-06) * norm_gain[None, :]).astype(jnp.bfloat16)
    capacity = max(2, 3 * tile_bins // (2 * expert_count))
    expert_col = expert_ids[:, 0]
    one_hot = (expert_col[:, None] == jnp.arange(expert_count, dtype=jnp.int32)[None, :]).astype(
        jnp.int32
    )
    within = jnp.sum(jnp.cumsum(one_hot, axis=0) * one_hot, axis=1) - 1
    slot_of = expert_col * capacity + within
    placer = (
        jnp.arange(expert_count * capacity, dtype=jnp.int32)[:, None] == slot_of[None, :]
    ).astype(jnp.bfloat16)
    outgoing = jnp.dot(placer, normed, preferred_element_type=jnp.float32).astype(jnp.bfloat16)
    arrived = lax.all_to_all(outgoing, "expert", split_axis=0, concat_axis=0, tiled=True)
    w_gate = dequantize(gate_q[0], gate_scales[0])
    w_up = dequantize(up_q[0], up_scales[0])
    w_down = dequantize(down_q[0], down_scales[0])
    contract = (((1,), (1,)), ((), ()))
    block_rows = lax.all_gather(arrived, "dp", axis=0, tiled=True)
    gate_val = lax.dot_general(block_rows, w_gate, contract, preferred_element_type=jnp.float32)
    up_val = lax.dot_general(block_rows, w_up, contract, preferred_element_type=jnp.float32)
    hidden = (jax.nn.silu(gate_val) * up_val).astype(jnp.bfloat16)
    partial_rows = jnp.dot(hidden, w_down, preferred_element_type=jnp.float32)
    summed = lax.psum_scatter(
        partial_rows.astype(jnp.bfloat16), "dp", scatter_dimension=0, tiled=True
    )
    returned = lax.all_to_all(summed, "expert", split_axis=0, concat_axis=0, tiled=True)
    expert_out = lax.dot_general(
        placer, returned, (((0,), (0,)), ((), ())), preferred_element_type=jnp.float32
    )
    return (residual_in + expert_out).astype(jnp.bfloat16)


def solution(mesh):
    placed = (
        P(("dp", "expert"), None),
        P(("dp", "expert")),
        P(("dp", "expert"), None),
        P(("dp", "expert"), None),
        P(),
        P(("dp", "expert"), None),
        P("expert", "dp", None),
        P("expert", "dp", None),
        P("expert", "dp", None),
        P("expert", "dp", None),
        P("expert", "dp", None),
        P("expert", "dp", None),
    )
    return jax.shard_map(
        on_device, mesh=mesh, in_specs=placed, out_specs=P(("dp", "expert"), None), check_vma=False
    )
```

profile of v0, /device:TPU:7, one launch (start us, length us, event | category | flops | bytes accessed | tf_op | source)
XLA Modules:
  0.0 243.5 jit_solution(11036003348992583538)
XLA Ops:
  6.5 0.9 reduce-window.8
  7.4 0.7 bitcast_subtract_fusion
  8.3 4.8 %gather_fusion = s32[768]{0:T(1024)S(1)} fusion(s32[256]{0:T(256)} %param.13, s32[1024]{0:T(1024)S(1)} %pad_clamp_fusion), kind=kCustom, calls=%fused_computation | custom fusion | bytes 9216 | tf_op jit(solution)/shard_map/jit(_take)/gather | solution.py:44
  13.2 0.7 select_select_fusion.1
  13.9 9.4 %all-to-all-start = ((s32[8,96,1]{1,2,0:T(1,128)}), s32[8,96,1]{1,2,0:T(1,128)S(1)}, u32[]{:S(2)}, u32[]{:S(2)}) async-start(s32[8,96,1]{1,2,0:T(1,128)} %bitcast.3), calls=%async_computation | async-start | bytes 8192 | tf_op jit(solution)/shard_map/all_to_all | solution.py:47
  23.3 2.8 %gather_fusion.1 = bf16[768,1024]{1,0:T(8,128)(2,1)S(1)} fusion(bf16[256,1024]{1,0:T(8,128)(2,1)S(1)} %copy-done, s32[1024]{0:T(1024)S(1)} %pad_clamp_fusion), kind=kCustom, calls=%fused_computation.1 | custom fusion | bytes 3148800 | tf_op jit(solution)/shard_map/jit(_take)/gather | solution.py:42
  26.2 1.5 select_select_fusion
  27.6 4.9 %all-to-all-start.1 = ((bf16[8,96,1024]{2,1,0:T(8,128)(2,1)}), bf16[8,96,1024]{2,1,0:T(8,128)(2,1)S(1)}, u32[]{:S(2)}, u32[]{:S(2)}) async-start(bf16[8,96,1024]{2,1,0:T(8,128)(2,1)} %select_select_fusion), calls=%async_computation.1 | async-start | bytes 3145728 | tf_op jit(solution)/shard_map/all_to_all | solution.py:46
  33.0 0.5 broadcast.229
  33.5 0.7 reduce.5
  34.3 17.3 %all-to-all-done.1 = bf16[8,96,1024]{2,1,0:T(8,128)(2,1)S(1)} async-done(((bf16[8,96,1024]{2,1,0:T(8,128)(2,1)}), bf16[8,96,1024]{2,1,0:T(8,128)(2,1)S(1)}, u32[]{:S(2)}, u32[]{:S(2)}) %all-to-all-start.1) | async-done | bytes 1572896 | tf_op jit(solution)/shard_map/all_to_all | solution.py:46
  51.6 0.5 multiply_reduce_fusion
  52.7 43.2 %all_to_all.39 = bf16[64,3,1024]{2,1,0:T(4,128)(2,1)S(1)} all-to-all(bf16[64,3,1024]{2,1,0:T(4,128)(2,1)S(1)} %all_to_all.29), channel_id=1, replica_groups=mesh['dp'=8,'expert'=64] {'expert'}, dimensions={0} | all-to-all | bytes 786432 | tf_op jit(solution)/shard_map/all_to_all | solution.py:65
  95.9 1.1 all_to_all.31
  97.3 29.6 %all-gather.2.cloned.1.call-done = bf16[1536,1024]{1,0:T(8,128)(2,1)} async-done(((bf16[192,1024]{1,0:T(8,128)(2,1)}), bf16[1536,1024]{1,0:T(8,128)(2,1)}) %all-gather.2.cloned.1.call-update) | async-done | bytes 3145744 | tf_op jit(solution)/shard_map/all_gather | solution.py:70
  127.0 0.6 broadcast_in_dim.67
  127.6 5.4 %fusion.5 = f32[1536,512]{1,0:T(8,128)} fusion(bf16[1536,1024]{1,0:T(8,128)(2,1)} %all-gather.2.cloned.1.call-done, bf16[64,8,8,128]{3,2,1,0:T(8,128)(2,1)S(1)} %bitcast.57, bf16[1,512,1024]{2,1,0:T(8,128)(2,1)S(1)} %copy-done.8), kind=kOutput, calls=%fused_computation.15 | convolution fusion | flops 1611137024 | bytes 8388608 | tf_op jit(solution)/shard_map/dot_general | solution.py:71
  133.1 0.6 broadcast_in_dim.69
  133.7 0.6 broadcast_in_dim.71
  134.3 8.9 %convolution_convert_fusion = bf16[1536,1024]{1,0:T(8,128)(2,1)} fusion(bf16[1536,1024]{1,0:T(8,128)(2,1)} %all-gather.2.cloned.1.call-done, f32[1536,512]{1,0:T(8,128)} %fusion.5, bf16[64,8,8,128]{3,2,1,0:T(8,128)(2,1)S(1)} %bitcast.56, bf16[64,8,8,128]{3,2,1,0:T(8,128)(2,1)S(1)} %bitcast.55, bf16[1,512,1024]{2,1,0:T(8,128)(2,1)} %param.20, ...), kind=kOutput, calls=%fused_computation.2 | convolution fusion | flops 3228565504 | bytes 13631488 | tf_op jit(solution)/shard_map/dot_general | solution.py:74
  143.3 43.7 %reduce-scatter.2.cloned.1.call-done = bf16[192,1024]{1,0:T(8,128)(2,1)} async-done(((bf16[1536,1024]{1,0:T(8,128)(2,1)}), bf16[192,1024]{1,0:T(8,128)(2,1)}) %reduce-scatter.2.cloned.1.call-update) | async-done | bytes 393232 | tf_op jit(solution)/shard_map/reduce_scatter | solution.py:75
  187.0 1.4 all_to_all.32
  188.4 46.9 %all_to_all.40 = bf16[64,3,1024]{2,1,0:T(4,128)(2,1)S(1)} all-to-all(bf16[64,3,1024]{2,1,0:T(4,128)(2,1)S(1)} %all_to_all.32), channel_id=1, replica_groups=mesh['dp'=8,'expert'=64] {'expert'}, dimensions={0} | all-to-all | bytes 786432 | tf_op jit(solution)/shard_map/all_to_all | solution.py:78
  235.6 1.0 fusion.1
  (44 shorter events, 2.1 us)
Async XLA Ops:
  6.5 16.8 %copy-start = (bf16[256,1024]{1,0:T(8,128)(2,1)S(1)}, bf16[256,1024]{1,0:T(8,128)(2,1)}, u32[]{:S(2)}) copy-start(bf16[256,1024]{1,0:T(8,128)(2,1)} %param.12) | copy-start | bytes 1572868
  6.5 6.6 %copy-start.7 = (s32[1,8]{1,0:T(1,128)S(1)}, s32[1,8]{1,0:T(1,128)}, u32[]{:S(2)}) copy-start(s32[1,8]{1,0:T(1,128)} %param.14) | copy-start | bytes 100
  13.9 13.8 %all-to-all-start = ((s32[8,96,1]{1,2,0:T(1,128)}), s32[8,96,1]{1,2,0:T(1,128)S(1)}, u32[]{:S(2)}, u32[]{:S(2)}) async-start(s32[8,96,1]{1,2,0:T(1,128)} %bitcast.3), calls=%async_computation | async-start | bytes 8192 | tf_op jit(solution)/shard_map/all_to_all | solution.py:47
  26.2 6.4 %copy-start.3 = (s32[128,1]{0,1:T(1,128)S(1)}, s32[128,1]{0,1:T(1,128)}, u32[]{:S(2)}) copy-start(s32[128,1]{0,1:T(1,128)} %param.17) | copy-start | bytes 1540
  26.2 25.4 %copy-start.1 = (bf16[128,1024]{1,0:T(8,128)(2,1)S(1)}, bf16[128,1024]{1,0:T(8,128)(2,1)}, u32[]{:S(2)}) copy-start(bf16[128,1024]{1,0:T(8,128)(2,1)} %param.15) | copy-start | bytes 786436
  27.6 24.4 %copy-start.2 = (f32[1024]{0:T(1024)S(1)}, f32[1024]{0:T(1024)}, u32[]{:S(2)}) copy-start(f32[1024]{0:T(1024)} %param.16) | copy-start | bytes 12292
  27.6 23.9 %all-to-all-start.1 = ((bf16[8,96,1024]{2,1,0:T(8,128)(2,1)}), bf16[8,96,1024]{2,1,0:T(8,128)(2,1)S(1)}, u32[]{:S(2)}, u32[]{:S(2)}) async-start(bf16[8,96,1024]{2,1,0:T(8,128)(2,1)} %select_select_fusion), calls=%async_computation.1 | async-start | bytes 3145728 | tf_op jit(solution)/shard_map/all_to_all | solution.py:46
  32.6 94.4 %all-gather.2.cloned.1.call-start = ((), (), s32[]{:S(2)}) async-start(), calls=%async_computation.5 | async-start | bytes 3538944 | tf_op jit(solution)/shard_map/all_gather | solution.py:70
  51.6 45.6 %copy-start.4 = (s32[1,4,8]{2,1,0:T(4,128)S(1)}, s32[1,4,8]{2,1,0:T(4,128)}, u32[]{:S(2)}) copy-start(s32[1,4,8]{2,1,0:T(4,128)} %param.21) | copy-start | bytes 388
  51.6 45.7 %copy-start.5 = (s32[1,4,8]{2,1,0:T(4,128)S(1)}, s32[1,4,8]{2,1,0:T(4,128)}, u32[]{:S(2)}) copy-start(s32[1,4,8]{2,1,0:T(4,128)} %param.22) | copy-start | bytes 388
  51.6 45.7 %copy-start.6 = (s32[1,4,8]{2,1,0:T(4,128)S(1)}, s32[1,4,8]{2,1,0:T(4,128)}, u32[]{:S(2)}) copy-start(s32[1,4,8]{2,1,0:T(4,128)} %param.23) | copy-start | bytes 388
  52.1 75.5 %copy-start.8 = (bf16[1,512,1024]{2,1,0:T(8,128)(2,1)S(1)}, bf16[1,512,1024]{2,1,0:T(8,128)(2,1)}, u32[]{:S(2)}) copy-start(bf16[1,512,1024]{2,1,0:T(8,128)(2,1)} %param.18) | copy-start | bytes 3145732
  97.0 90.0 %reduce-scatter.2.cloned.1.call-start = ((), (), s32[]{:S(2)}) async-start(), calls=%async_computation.6 | async-start | bytes 3538944 | tf_op jit(solution)/shard_map/reduce_scatter | solution.py:75
Sparse Core Ops, SparseCore 0:
  97.1 29.7 all-gather.1
  143.4 43.5 reduce-scatter.1
where the time goes:
time: 244 us; the launch traced here: 243 us
  waiting for transfers between devices  90.7 us (37%)
  blocking collectives  90.1 us (37%)
  matrix products  16.2 us (7%)
  starting transfers between devices  14.6 us (6%)
  between operations  13.6 us (6%)
  local copies, waits for them, and re-layouts  13.3 us (5%)
  other arithmetic  4.98 us (2%)
    all_to_all x1, blocking collectives, on_device(): lax.all_to_all(summed, 'expert', split_axis=0, concat_axis=0, tiled=True)  46.9 us
    reduce_scatter x1, waiting for transfers between devices, on_device(): lax.psum_scatter(partial_rows.astype(jnp.bfloat16), 'dp', scatter_dimensi...  43.7 us
    all_to_all x1, blocking collectives, on_device(): lax.all_to_all(outgoing, 'expert', split_axis=0, concat_axis=0, tiled=True)  43.2 us
    all_gather x1, waiting for transfers between devices, on_device(): block_rows = lax.all_gather(arrived, 'dp', axis=0, tiled=True)  29.6 us
    all_to_all x1, waiting for transfers between devices, on_device(): lax.all_to_all(slot_rows, 'dp', split_axis=0, concat_axis=0, tiled=True)  17.3 us
    all_to_all x1, starting transfers between devices, on_device(): lax.all_to_all(slot_bins, 'dp', split_axis=0, concat_axis=0, tiled=True)  9.41 us
    dot_general x1, matrix products, on_device(): partial_rows = jnp.dot(hidden, w_down, preferred_element_type=jnp.float32)  8.93 us
    dot_general x1, matrix products, on_device(): lax.dot_general(block_rows, w_gate, contract, preferred_element_type=jnp....  5.44 us
  transfers between devices with their start and end apart: 4, of which 3 were waited for; matrix products, arithmetic and copies ran while one was open for 2% of the time, Pallas kernels for 0%

commit v1 on v0

--- a/solution.py
+++ b/solution.py
@@ -1,9 +1,20 @@
+import functools
 import jax
 import jax.numpy as jnp
 from jax import lax
 from jax.sharding import PartitionSpec as P
+from jax.lax import all_to_all, axis_size
 
 QB = 128
+
+
+def divide_squares_over_axis(values, row_axis):
+    return jnp.concatenate(
+        all_to_all(jnp.stack([values for _ in range(axis_size(row_axis))], 0), row_axis, 0, 0), 0
+    )
+
+
+streams_plan = functools.partial(divide_squares_over_axis, row_axis="dp")
 
 
 def dequantize(quant, scale):
@@ -67,7 +78,7 @@
     w_up = dequantize(up_q[0], up_scales[0])
     w_down = dequantize(down_q[0], down_scales[0])
     contract = (((1,), (1,)), ((), ()))
-    block_rows = lax.all_gather(arrived, "dp", axis=0, tiled=True)
+    block_rows = streams_plan(arrived)
     gate_val = lax.dot_general(block_rows, w_gate, contract, preferred_element_type=jnp.float32)
     up_val = lax.dot_general(block_rows, w_up, contract, preferred_element_type=jnp.float32)
     hidden = (jax.nn.silu(gate_val) * up_val).astype(jnp.bfloat16)

time: 244 us -> 252 us (1.033)
  starting transfers between devices: 14.6 us -> 25 us
  waiting for transfers between devices: 90.7 us -> 84.4 us
  local copies, waits for them, and re-layouts: 13.3 us -> 16.5 us
    all_to_all x0 -> x1, waiting for transfers between devices: none -> 32.8 us  [divide_squares_over_axis(): all_to_all(jnp.stack([values for _ in range(axis_size(row_axis))], 0), ro...]
    all_gather x1 -> x0, waiting for transfers between devices: 29.6 us -> none  [on_device(): block_rows = lax.all_gather(arrived, 'dp', axis=0, tiled=True)]
    all_to_all x0 -> x1, starting transfers between devices: none -> 10.7 us  [divide_squares_over_axis(): all_to_all(jnp.stack([values for _ in range(axis_size(row_axis))], 0), ro...]
    reduce_scatter x1, waiting for transfers between devices: 43.7 us -> 34.3 us  [on_device(): lax.psum_scatter(partial_rows.astype(jnp.bfloat16), 'dp', scatter_dimensi...]
  transfers between devices with their start and end apart: 4 -> 4, of which waited for: 3 -> 3; matrix products, arithmetic and copies ran while one was open for 2% -> 4% of each run, Pallas kernels for 0% -> 0%
where the time goes in v1:
time: 252 us; the launch traced here: 251 us
  blocking collectives  90.2 us (36%)
  waiting for transfers between devices  84.4 us (33%)
  starting transfers between devices  25 us (10%)
  local copies, waits for them, and re-layouts  16.5 us (7%)
  matrix products  16.5 us (7%)
  between operations  13.6 us (5%)
  other arithmetic  4.98 us (2%)
    all_to_all x1, blocking collectives, on_device(): lax.all_to_all(summed, 'expert', split_axis=0, concat_axis=0, tiled=True)  46.9 us
    all_to_all x1, blocking collectives, on_device(): lax.all_to_all(outgoing, 'expert', split_axis=0, concat_axis=0, tiled=True)  43.2 us
    reduce_scatter x1, waiting for transfers between devices, on_device(): lax.psum_scatter(partial_rows.astype(jnp.bfloat16), 'dp', scatter_dimensi...  34.3 us
    all_to_all x1, waiting for transfers between devices, divide_squares_over_axis(): all_to_all(jnp.stack([values for _ in range(axis_size(row_axis))], 0), ro...  32.8 us
    all_to_all x1, waiting for transfers between devices, on_device(): lax.all_to_all(slot_rows, 'dp', split_axis=0, concat_axis=0, tiled=True)  17.3 us
    all_to_all x1, starting transfers between devices, divide_squares_over_axis(): all_to_all(jnp.stack([values for _ in range(axis_size(row_axis))], 0), ro...  10.7 us
    all_to_all x1, starting transfers between devices, on_device(): lax.all_to_all(slot_bins, 'dp', split_axis=0, concat_axis=0, tiled=True)  9.41 us
    dot_general x1, matrix products, on_device(): partial_rows = jnp.dot(hidden, w_down, preferred_element_type=jnp.float32)  8.91 us
  transfers between devices with their start and end apart: 4, of which 3 were waited for; matrix products, arithmetic and copies ran while one was open for 4% of the time, Pallas kernels for 0%

profile of v1, /device:TPU:7, one launch (start us, length us, event | category | flops | bytes accessed | tf_op | source)
XLA Modules:
  0.0 251.2 jit_solution(17387987381864511917)
XLA Ops:
  6.5 0.9 reduce-window.8
  7.4 0.7 bitcast_subtract_fusion
  8.3 4.8 %gather_fusion = s32[768]{0:T(1024)S(1)} fusion(s32[256]{0:T(256)} %param.13, s32[1024]{0:T(1024)S(1)} %pad_clamp_fusion), kind=kCustom, calls=%fused_computation | custom fusion | bytes 9216 | tf_op jit(solution)/shard_map/jit(_take)/gather | solution.py:55
  13.2 0.7 select_select_fusion.1
  13.9 9.4 %all-to-all-start = ((s32[8,96,1]{1,2,0:T(1,128)}), s32[8,96,1]{1,2,0:T(1,128)S(1)}, u32[]{:S(2)}, u32[]{:S(2)}) async-start(s32[8,96,1]{1,2,0:T(1,128)} %bitcast.3), calls=%async_computation | async-start | bytes 8192 | tf_op jit(solution)/shard_map/all_to_all | solution.py:58
  23.3 2.8 %gather_fusion.1 = bf16[768,1024]{1,0:T(8,128)(2,1)S(1)} fusion(bf16[256,1024]{1,0:T(8,128)(2,1)S(1)} %copy-done, s32[1024]{0:T(1024)S(1)} %pad_clamp_fusion), kind=kCustom, calls=%fused_computation.1 | custom fusion | bytes 3148800 | tf_op jit(solution)/shard_map/jit(_take)/gather | solution.py:53
  26.2 1.5 select_select_fusion
  27.6 4.9 %all-to-all-start.1 = ((bf16[8,96,1024]{2,1,0:T(8,128)(2,1)}), bf16[8,96,1024]{2,1,0:T(8,128)(2,1)S(1)}, u32[]{:S(2)}, u32[]{:S(2)}) async-start(bf16[8,96,1024]{2,1,0:T(8,128)(2,1)} %select_select_fusion), calls=%async_computation.1 | async-start | bytes 3145728 | tf_op jit(solution)/shard_map/all_to_all | solution.py:57
  33.5 0.7 reduce.5
  34.3 17.3 %all-to-all-done.1 = bf16[8,96,1024]{2,1,0:T(8,128)(2,1)S(1)} async-done(((bf16[8,96,1024]{2,1,0:T(8,128)(2,1)}), bf16[8,96,1024]{2,1,0:T(8,128)(2,1)S(1)}, u32[]{:S(2)}, u32[]{:S(2)}) %all-to-all-start.1) | async-done | bytes 1572896 | tf_op jit(solution)/shard_map/all_to_all | solution.py:57
  52.6 43.2 %all_to_all.41 = bf16[64,3,1024]{2,1,0:T(4,128)(2,1)S(1)} all-to-all(bf16[64,3,1024]{2,1,0:T(4,128)(2,1)S(1)} %all_to_all.30), channel_id=1, replica_groups=mesh['dp'=8,'expert'=64] {'expert'}, dimensions={0} | all-to-all | bytes 786432 | tf_op jit(solution)/shard_map/all_to_all | solution.py:76
  96.2 2.1 stack.5
  98.3 10.7 %all-to-all-start.3 = ((bf16[8,192,1024]{2,1,0:T(8,128)(2,1)}), bf16[8,192,1024]{2,1,0:T(8,128)(2,1)}, u32[]{:S(2)}, u32[]{:S(2)}) async-start(bf16[8,192,1024]{2,1,0:T(8,128)(2,1)} %stack.5), calls=%async_computation.3 | async-start | bytes 6291456 | tf_op jit(solution)/shard_map/all_to_all | solution.py:13
  109.1 0.6 broadcast_in_dim.67
  110.2 0.6 broadcast_in_dim.69
  110.8 1.3 convert_element_type.104
  112.1 32.8 %all-to-all-done.3 = bf16[8,192,1024]{2,1,0:T(8,128)(2,1)} async-done(((bf16[8,192,1024]{2,1,0:T(8,128)(2,1)}), bf16[8,192,1024]{2,1,0:T(8,128)(2,1)}, u32[]{:S(2)}, u32[]{:S(2)}) %all-to-all-start.3) | async-done | bytes 3145760 | tf_op jit(solution)/shard_map/all_to_all | solution.py:13
  144.9 5.8 %fusion.6 = f32[1536,512]{1,0:T(8,128)} fusion(bf16[1536,1024]{1,0:T(8,128)(2,1)} %bitcast.7, bf16[1,512,1024]{2,1,0:T(8,128)(2,1)} %param.18, bf16[1,512,1024]{2,1,0:T(8,128)(2,1)S(1)} %convert_element_type.99), kind=kOutput, calls=%fused_computation.14 | convolution fusion | flops 1611137024 | bytes 8388608 | tf_op jit(solution)/shard_map/dot_general | solution.py:82
  150.8 0.6 broadcast_in_dim.71
  151.4 8.9 %convolution_convert_fusion = bf16[1536,1024]{1,0:T(8,128)(2,1)} fusion(bf16[1536,1024]{1,0:T(8,128)(2,1)} %bitcast.7, f32[1536,512]{1,0:T(8,128)} %fusion.6, bf16[64,8,8,128]{3,2,1,0:T(8,128)(2,1)S(1)} %bitcast.43, bf16[1,512,1024]{2,1,0:T(8,128)(2,1)} %param.20, bf16[1,512,1024]{2,1,0:T(8,128)(2,1)} %param.19, bf16[1,512,1024]{2,1,0:T(8,128)(2,1)S(1)} %copy-done.1), kind=kOutput, calls=%fused_computation.2 | convolution fusion | flops 3228565504 | bytes 13631488 | tf_op jit(solution)/shard_map/dot_general | solution.py:85
  160.3 34.3 %reduce-scatter.2.cloned.1.call-done = bf16[192,1024]{1,0:T(8,128)(2,1)} async-done(((bf16[1536,1024]{1,0:T(8,128)(2,1)}), bf16[192,1024]{1,0:T(8,128)(2,1)}) %reduce-scatter.2.cloned.1.call-update) | async-done | bytes 393232 | tf_op jit(solution)/shard_map/reduce_scatter | solution.py:86
  194.6 1.4 all_to_all.33
  196.1 46.9 %all_to_all.42 = bf16[64,3,1024]{2,1,0:T(4,128)(2,1)S(1)} all-to-all(bf16[64,3,1024]{2,1,0:T(4,128)(2,1)S(1)} %all_to_all.33), channel_id=1, replica_groups=mesh['dp'=8,'expert'=64] {'expert'}, dimensions={0} | all-to-all | bytes 786432 | tf_op jit(solution)/shard_map/all_to_all | solution.py:89
  243.3 1.0 fusion.1
  (46 shorter events, 3.7 us)
Async XLA Ops:
  6.5 16.8 %copy-start = (bf16[256,1024]{1,0:T(8,128)(2,1)S(1)}, bf16[256,1024]{1,0:T(8,128)(2,1)}, u32[]{:S(2)}) copy-start(bf16[256,1024]{1,0:T(8,128)(2,1)} %param.12) | copy-start | bytes 1572868
  6.5 6.6 %copy-start.8 = (s32[1,8]{1,0:T(1,128)S(1)}, s32[1,8]{1,0:T(1,128)}, u32[]{:S(2)}) copy-start(s32[1,8]{1,0:T(1,128)} %param.14) | copy-start | bytes 100
  13.9 13.8 %all-to-all-start = ((s32[8,96,1]{1,2,0:T(1,128)}), s32[8,96,1]{1,2,0:T(1,128)S(1)}, u32[]{:S(2)}, u32[]{:S(2)}) async-start(s32[8,96,1]{1,2,0:T(1,128)} %bitcast.3), calls=%async_computation | async-start | bytes 8192 | tf_op jit(solution)/shard_map/all_to_all | solution.py:58
  26.2 6.4 %copy-start.4 = (s32[128,1]{0,1:T(1,128)S(1)}, s32[128,1]{0,1:T(1,128)}, u32[]{:S(2)}) copy-start(s32[128,1]{0,1:T(1,128)} %param.17) | copy-start | bytes 1540
  26.2 25.4 %copy-start.2 = (bf16[128,1024]{1,0:T(8,128)(2,1)S(1)}, bf16[128,1024]{1,0:T(8,128)(2,1)}, u32[]{:S(2)}) copy-start(bf16[128,1024]{1,0:T(8,128)(2,1)} %param.15) | copy-start | bytes 786436
  27.6 24.4 %copy-start.3 = (f32[1024]{0:T(1024)S(1)}, f32[1024]{0:T(1024)}, u32[]{:S(2)}) copy-start(f32[1024]{0:T(1024)} %param.16) | copy-start | bytes 12292
  27.6 23.9 %all-to-all-start.1 = ((bf16[8,96,1024]{2,1,0:T(8,128)(2,1)}), bf16[8,96,1024]{2,1,0:T(8,128)(2,1)S(1)}, u32[]{:S(2)}, u32[]{:S(2)}) async-start(bf16[8,96,1024]{2,1,0:T(8,128)(2,1)} %select_select_fusion), calls=%async_computation.1 | async-start | bytes 3145728 | tf_op jit(solution)/shard_map/all_to_all | solution.py:57
  98.3 10.7 %copy-start.5 = (s32[1,4,8]{2,1,0:T(4,128)S(1)}, s32[1,4,8]{2,1,0:T(4,128)}, u32[]{:S(2)}) copy-start(s32[1,4,8]{2,1,0:T(4,128)} %param.21) | copy-start | bytes 388
  98.3 46.6 %all-to-all-start.3 = ((bf16[8,192,1024]{2,1,0:T(8,128)(2,1)}), bf16[8,192,1024]{2,1,0:T(8,128)(2,1)}, u32[]{:S(2)}, u32[]{:S(2)}) async-start(bf16[8,192,1024]{2,1,0:T(8,128)(2,1)} %stack.5), calls=%async_computation.3 | async-start | bytes 6291456 | tf_op jit(solution)/shard_map/all_to_all | solution.py:13
  109.0 1.2 copy-start.6
  109.0 85.6 %reduce-scatter.2.cloned.1.call-start = ((), (), s32[]{:S(2)}) async-start(), calls=%async_computation.6 | async-start | bytes 3538944 | tf_op jit(solution)/shard_map/reduce_scatter | solution.py:86
  109.0 3.1 %copy-start.7 = (s32[1,4,8]{2,1,0:T(4,128)S(1)}, s32[1,4,8]{2,1,0:T(4,128)}, u32[]{:S(2)}) copy-start(s32[1,4,8]{2,1,0:T(4,128)} %param.23) | copy-start | bytes 388
  144.9 6.4 %copy-start.1 = (bf16[1,512,1024]{2,1,0:T(8,128)(2,1)S(1)}, bf16[1,512,1024]{2,1,0:T(8,128)(2,1)}, u32[]{:S(2)}) copy-start(bf16[1,512,1024]{2,1,0:T(8,128)(2,1)} %convert_element_type.104) | copy-start | bytes 3145732
Sparse Core Ops, SparseCore 0:
  160.4 34.1 reduce-scatter.1
